TPU v7x, 32 devices: a whole 2x2x4 slice. The times are simulated.
32 devices in a mesh: lat: 4 (over x, core), lon: 8 (over z, y).
Axes of the slice: x: 2, y: 2, z: 4, core: 2. Of those that a mesh axis runs over, the one named last changes fastest.
Arguments:
- field: bfloat16 [64, 256, 1024], P('lat', 'lon'), may hold values from -600 to 600
- norm_gain: float32 [1024], replicated, may hold values from 0.1 to 1.9
- w_qkv: bfloat16 [1024, 3072], replicated, may hold values from -2 to 2
- w_out: bfloat16 [1024, 1024], replicated, may hold values from -0.1875 to 0.1875
- block_cols: int32 [4, 4], replicated, may hold values from 1 to 7, as said below
- antipode: int32 [256], P('lon'), may hold values from 0 to 255, as said below
Outputs:
- update: bfloat16 [64, 256, 1024], P('lat', 'lon')
Inputs may be any that keep to these rules, and one draw needn't show every extreme that they name: `block_cols`: each row lists 4 different blocks b with |b - 4 - row| <= 3. A permutation of the longitudes; antipode[l] // 32 equals (l // 32 + 256 // 64) modulo 256 // 32.
All inputs are finite; a program needn't handle non-finite values.
Results may differ from a plain program's by a relative error of at most 0.005.
The roundings to bfloat16 on the way count: a program that leaves them out, or rounds other values in their place, can miss the bound.
Values may be sent and summed in bfloat16 or wider, within the bound.
A program may use at most 128 MiB of HBM per device.

v0:
```python
import jax
import jax.numpy as jnp
from jax import lax
from jax.sharding import PartitionSpec as P

HEADS = 16
HD = 64
HZ = 8
BM = 8
epsilon = 1e-06


def shifted(shard, axis, by):
    devices = lax.axis_size(axis)
    return lax.ppermute(shard, axis, [(i, (i + by) % devices) for i in range(devices)])


def from_partner(value, axis, distance):
    mask = 2**distance
    pairs = [(source, source ^ mask) for source in range(lax.axis_size(axis))]
    return lax.ppermute(value, axis, pairs)


def softmax_rows(scores):
    row_max = jnp.max(scores, axis=-1, keepdims=True)
    exponent = jnp.exp(scores - row_max)
    return (exponent / jnp.sum(exponent, axis=-1, keepdims=True)).astype(jnp.bfloat16)


def zonal_attend(query_rows, key_rows, value_rows):
    item_count, length, pair_width = query_rows.shape
    score_scale = HD ** (-0.5)
    query_heads = query_rows.reshape(item_count, length, 2, HD)
    key_heads = key_rows.reshape(item_count, length, 2, HD)
    value_heads = value_rows.reshape(item_count, length, 2, HD)
    block_rows = min(512, length)
    pieces = []
    for first_row in range(0, length, block_rows):
        query_block = query_heads[:, first_row : first_row + block_rows]
        scores = (
            jnp.einsum(
                "iqhd,ikhd->ihqk", query_block, key_heads, preferred_element_type=jnp.float32
            )
            * score_scale
        )
        soft_weights = softmax_rows(scores)
        result = jnp.einsum(
            "ihqk,ikhd->iqhd", soft_weights, value_heads, preferred_element_type=jnp.float32
        )
        pieces.append(result.astype(jnp.bfloat16))
    return jnp.concatenate(pieces, axis=1).reshape(item_count, length, pair_width)


def on_device(field, norm_gain, w_qkv, w_out, block_cols, antipode):
    cycle_count, lon_count, channels = field.shape
    column_heads = HEADS - HZ
    pair_count = HZ // 2
    zonal_width = HZ * HD
    score_scale = HD ** (-0.5)
    values = field.astype(jnp.float32)
    scaled = values * lax.rsqrt(jnp.mean(values * values, axis=-1, keepdims=True) + epsilon)
    normed = (scaled * norm_gain).astype(jnp.bfloat16)
    weight_split = w_qkv.reshape(channels, 3, channels)
    zonal_weight = weight_split[:, :, :zonal_width].reshape(channels, 3, pair_count, 2 * HD)
    column_weight = weight_split[:, :, zonal_width:]
    zonal_part = jnp.einsum(
        "rld,dtpc->trplc", normed, zonal_weight, preferred_element_type=jnp.float32
    )
    zonal_part = zonal_part.astype(jnp.bfloat16).reshape(
        3, cycle_count * pair_count, lon_count, 2 * HD
    )
    column_proj = jnp.einsum(
        "rld,dtc->rltc", normed, column_weight, preferred_element_type=jnp.float32
    ).astype(jnp.bfloat16)
    query_all, key_all, value_all = (
        lax.all_to_all(zonal_part[0], "lon", split_axis=0, concat_axis=1, tiled=True),
        lax.all_to_all(zonal_part[1], "lon", split_axis=0, concat_axis=1, tiled=True),
        lax.all_to_all(zonal_part[2], "lon", split_axis=0, concat_axis=1, tiled=True),
    )
    zonal_items = zonal_attend(query_all, key_all, value_all)
    returned = lax.all_to_all(zonal_items, "lon", split_axis=1, concat_axis=0, tiled=True)
    zonal_out = returned.reshape(cycle_count, pair_count, lon_count, 2 * HD)
    cap_half = lax.axis_index("lat") % 2
    lon_devices = lax.axis_size("lon")
    merged = column_proj[:, :, 1:]

    def cap_order(own_rows, other_rows):
        return jnp.where(
            cap_half == 0,
            jnp.concatenate([own_rows, other_rows], axis=0),
            jnp.concatenate([other_rows, own_rows], axis=0),
        )

    far_own = shifted(merged, "lon", lon_devices // 2)
    partner, far_partner = from_partner((merged, far_own), "lat", 0)
    cap_rows = cap_order(merged, partner)
    far_side = cap_order(far_own, far_partner)
    across = jnp.take(far_side, antipode % lon_count, axis=1)[::-1]
    column = jnp.concatenate([across, cap_rows], axis=0)
    block_total = column.shape[0] // BM
    column = column.reshape(block_total, BM, lon_count, 2, column_heads, HD)
    picks_per_row = block_cols.shape[1]
    local_blocks = cycle_count // BM
    pieces = []
    for local_block in range(local_blocks):
        block_row = cap_half * local_blocks + local_block
        picked = lax.dynamic_index_in_dim(block_cols, block_row, 0, keepdims=False)
        chosen = jnp.take(column, picked, axis=0).reshape(
            picks_per_row * BM, lon_count, 2, column_heads, HD
        )
        query_block = column_proj[local_block * BM : (local_block + 1) * BM, :, 0]
        query_block = query_block.reshape(BM, lon_count, column_heads, HD)
        scores = (
            jnp.einsum(
                "qlhd,klhd->lhqk", query_block, chosen[:, :, 0], preferred_element_type=jnp.float32
            )
            * score_scale
        )
        soft_weights = softmax_rows(scores)
        result = jnp.einsum(
            "lhqk,klhd->qlhd", soft_weights, chosen[:, :, 1], preferred_element_type=jnp.float32
        )
        pieces.append(result.astype(jnp.bfloat16).reshape(BM, lon_count, column_heads * HD))
    meridional = jnp.concatenate(pieces, axis=0)
    zonal_rows_out = w_out[:zonal_width].reshape(pair_count, 2 * HD, channels)
    total = jnp.einsum(
        "rplc,pce->rle", zonal_out, zonal_rows_out, preferred_element_type=jnp.float32
    )
    total = total + jnp.einsum(
        "rlc,ce->rle", meridional, w_out[zonal_width:], preferred_element_type=jnp.float32
    )
    return total.astype(jnp.bfloat16)


def solution(mesh):
    in_specs = (P("lat", "lon", None), P(), P(), P(), P(), P("lon"))
    out_specs = P("lat", "lon", None)
    return jax.shard_map(
        on_device, mesh=mesh, in_specs=in_specs, out_specs=out_specs, check_vma=False
    )
```

profile of v0, /device:TPU:1, one launch (start us, length us, event | category | flops | bytes accessed | tf_op | source)
XLA Modules:
  0.0 214.1 jit_solution(12262498181520285386)
XLA Ops:
  0.0 1.5 fusion.7
  1.5 8.6 %copy.53 = bf16[1024,3072]{0,1:T(8,128)(2,1)} copy(bf16[1024,3072]{1,0:T(8,128)(2,1)} %param.10) | data formatting | bytes 12582912 | tf_op args[2]
  10.1 2.3 %slice.65 = bf16[1024,3,512]{0,2,1:T(8,128)(2,1)S(1)} slice(bf16[1024,3,1024]{0,2,1:T(8,128)(2,1)} %bitcast.123), slice={[0:1024], [0:3], [0:512]} | slice | bytes 6291456 | tf_op jit(solution)/shard_map/slice | solution.py:64
  12.4 0.0 copy-done.5
  12.4 0.0 copy-done.7
  12.4 1.9 fusion.19
  14.4 1.1 fusion.52
  15.5 19.8 %all_to_all.60 = bf16[64,32,128]{2,1,0:T(8,128)(2,1)S(1)} all-to-all(bf16[64,32,128]{2,1,0:T(8,128)(2,1)S(1)} %bitcast.137), channel_id=1, replica_groups=mesh['lat'=4,'lon'=8] {'lon'}, dimensions={0} | all-to-all | bytes 1048576 | tf_op jit(solution)/shard_map/all_to_all | solution.py:77
  35.3 17.5 %all_to_all.61 = bf16[64,32,128]{2,1,0:T(8,128)(2,1)S(1)} all-to-all(bf16[64,32,128]{2,1,0:T(8,128)(2,1)S(1)} %bitcast.136), channel_id=1, replica_groups=mesh['lat'=4,'lon'=8] {'lon'}, dimensions={0} | all-to-all | bytes 1048576 | tf_op jit(solution)/shard_map/all_to_all | solution.py:78
  52.8 4.1 %all-to-all-start.1 = ((bf16[64,32,128]{2,1,0:T(8,128)(2,1)}), bf16[64,32,128]{2,1,0:T(8,128)(2,1)S(1)}, u32[]{:S(2)}, u32[]{:S(2)}) async-start(bf16[64,32,128]{2,1,0:T(8,128)(2,1)} %bitcast.9), calls=%async_computation.1 | async-start | bytes 1048576 | tf_op jit(solution)/shard_map/all_to_all | solution.py:76
  56.9 3.8 %fusion.18 = bf16[16,32,3,512]{3,1,2,0:T(8,128)(2,1)S(1)} fusion(bf16[1024,3,1024]{0,2,1:T(8,128)(2,1)} %bitcast.124, bf16[16,32,1024]{2,1,0:T(8,128)(2,1)S(1)} %copy-done.5, f32[1024]{0:T(1024)S(1)} %copy-done.7, f32[16,32]{1,0:T(8,128)S(1)} %add_rsqrt_fusion), kind=kOutput, calls=%fused_computation.38 | convolution fusion | flops 1613496320 | bytes 5773312 | tf_op jit(solution)/shard_map/rld,dtc->rltc/dot_general | solution.py:72
  60.7 0.0 copy-start.3
  60.7 0.1 slice.70
  60.8 1.4 collective-permute-start.2
  62.3 2.6 %collective-permute-start = (bf16[16,32,2,512]{3,1,2,0:T(8,128)(2,1)S(1)}, bf16[16,32,2,512]{3,1,2,0:T(8,128)(2,1)}, u32[]{:S(2)}, u32[]{:S(2)}) collective-permute-start(bf16[16,32,2,512]{3,1,2,0:T(8,128)(2,1)S(1)} %slice.70), channel_id=1, source_target_pairs={{0,4},{1,5},{2,6},{3,7},{4,0},{5,1},{6,2},{7,3},{8,12},{9,13},{10,... | collective-permute-start | bytes 3145736 | tf_op jit(solution)/shard_map/ppermute | solution.py:15
  64.9 0.8 copy.57
  65.8 0.0 copy-done.3
  65.8 26.7 %all-to-all-done.1 = bf16[64,32,128]{2,1,0:T(8,128)(2,1)S(1)} async-done(((bf16[64,32,128]{2,1,0:T(8,128)(2,1)}), bf16[64,32,128]{2,1,0:T(8,128)(2,1)S(1)}, u32[]{:S(2)}, u32[]{:S(2)}) %all-to-all-start.1) | async-done | bytes 524320 | tf_op jit(solution)/shard_map/all_to_all | solution.py:76
  92.5 0.4 reshape.78
  92.9 1.4 reshape.77
  94.3 2.4 %reshape.79 = bf16[8,256,2,64]{3,2,1,0:T(2,128)(2,1)S(1)} reshape(bf16[8,8,32,128]{3,2,1,0:T(8,128)(2,1)} %copy.57) | data formatting | bytes 1048576 | tf_op jit(solution)/shard_map/reshape | solution.py:34
  96.8 0.7 fusion.36
  97.5 0.0 copy-start.4
  97.5 3.2 %fusion.56 = (f32[8,2,256]{2,1,0:T(2,128)S(1)}, f32[8,2,256,256]{2,3,1,0:T(8,128)S(1)}) fusion(f32[8,2,256,256]{2,3,1,0:T(8,128)S(1)} %fusion.36), kind=kOutput, calls=%fused_computation.90 | output fusion | flops 4194559 | bytes 8404992 | tf_op jit(solution)/shard_map/sub | solution.py:26
  100.8 0.0 copy-done.4
  100.8 0.5 fusion.28
  101.3 1.1 copy.62
  102.4 5.0 %all-to-all-start.3 = ((bf16[8,256,128]{2,0,1:T(8,128)(2,1)}), bf16[8,256,128]{2,0,1:T(8,128)(2,1)S(1)}, u32[]{:S(2)}, u32[]{:S(2)}) async-start(bf16[8,256,128]{2,0,1:T(8,128)(2,1)} %copy.62), calls=%async_computation.3 | async-start | bytes 1048576 | tf_op jit(solution)/shard_map/all_to_all | solution.py:81
  107.3 13.7 %collective-permute-done = bf16[16,32,2,512]{3,1,2,0:T(8,128)(2,1)} collective-permute-done((bf16[16,32,2,512]{3,1,2,0:T(8,128)(2,1)S(1)}, bf16[16,32,2,512]{3,1,2,0:T(8,128)(2,1)}, u32[]{:S(2)}, u32[]{:S(2)}) %collective-permute-start) | collective-permute-done | bytes 1048608 | tf_op jit(solution)/shard_map/ppermute | solution.py:15
  121.0 3.8 %collective-permute-start.1 = (bf16[16,32,2,512]{3,1,2,0:T(8,128)(2,1)}, bf16[16,32,2,512]{3,1,2,0:T(8,128)(2,1)}, u32[]{:S(2)}, u32[]{:S(2)}) collective-permute-start(bf16[16,32,2,512]{3,1,2,0:T(8,128)(2,1)} %collective-permute-done), channel_id=1, source_target_pairs={{0,8},{8,0},{16,24},{24,16},{1,9},{9,1},{17,25},{25,17},{2,10},{10... | collective-permute-start | bytes 3145736 | tf_op jit(solution)/shard_map/ppermute | solution.py:21
  124.8 1.1 fusion.53
  125.9 0.0 copy-start.6
  125.9 0.0 copy-start.8
  125.9 0.3 reshape_squeeze.6
  126.2 0.3 reshape_squeeze.7
  126.5 0.1 copy-done.6
  126.6 0.0 copy-done.8
  126.7 0.0 collective-permute-done.2
  126.7 3.2 %maximum_select_fusion.1 = bf16[32,32,2,512]{3,1,2,0:T(8,128)(2,1)} fusion(bf16[16,32,2,512]{3,1,2,0:T(8,128)(2,1)} %collective-permute-done.2, bf16[16,32,2,512]{3,1,2,0:T(8,128)(2,1)S(1)} %slice.70, pred[]{:T(512)S(6)} %eq.8), kind=kLoop, calls=%fused_computation.31 | loop fusion | flops 3145728 | bytes 4194305 | tf_op jit(solution)/shard_map/jit(_where)/select_n | solution.py:88
  129.9 0.0 all-to-all-done.3
  129.9 0.9 copy.64
  130.8 0.0 collective-permute-done.1
  130.8 2.6 %maximum_select_fusion = bf16[32,32,2,512]{3,1,2,0:T(8,128)(2,1)S(1)} fusion(bf16[16,32,2,512]{3,1,2,0:T(8,128)(2,1)} %collective-permute-done.1, bf16[16,32,2,512]{3,1,2,0:T(8,128)(2,1)} %collective-permute-done, pred[]{:T(512)S(6)} %eq.8), kind=kLoop, calls=%fused_computation.30 | loop fusion | flops 3145728 | bytes 4194305 | tf_op jit(solution)/shard_map/jit(_where)/select_n | solution.py:88
  133.4 2.5 %copy.66 = bf16[32,32,2,512]{3,0,2,1:T(8,128)(2,1)} copy(bf16[32,32,2,512]{3,1,2,0:T(8,128)(2,1)S(1)} %maximum_select_fusion) | data formatting | bytes 4194304 | tf_op jit(solution)/shard_map/jit(_where)/select_n | solution.py:88
  135.8 2.3 %gather_fusion = bf16[32,32,2,512]{3,1,2,0:T(8,128)(2,1)S(1)} fusion(bf16[32,32,2,512]{3,0,2,1:T(8,128)(2,1)} %copy.66, s32[1024]{0:T(1024)S(1)} %pad_clamp_fusion.2), kind=kCustom, calls=%fused_computation.2 | custom fusion | bytes 4194432 | tf_op jit(solution)/shard_map/jit(_take)/gather | solution.py:98
  138.1 3.8 %fusion.15 = bf16[32,32,2,512]{3,1,2,0:T(8,128)(2,1)} fusion(bf16[32,32,2,512]{3,1,2,0:T(8,128)(2,1)S(1)} %gather_fusion, pred[32]{0:T(512)(128)(4,1)S(1)} %get-tuple-element.10), kind=kLoop, calls=%fused_computation.35 | loop fusion | flops 1048576 | bytes 4194336 | tf_op jit(solution)/shard_map/jit(_take)/select_n | solution.py:98
  141.9 3.3 %rev.3 = bf16[32,32,2,512]{3,1,2,0:T(8,128)(2,1)} reverse(bf16[32,32,2,512]{3,1,2,0:T(8,128)(2,1)} %fusion.15), dimensions={0} | reverse | bytes 4194304 | tf_op jit(solution)/shard_map/rev | solution.py:98
  145.2 3.9 %pad_maximum_fusion = bf16[64,32,2,512]{3,1,2,0:T(8,128)(2,1)} fusion(bf16[32,32,2,512]{3,1,2,0:T(8,128)(2,1)S(1)} %copy-done, bf16[32,32,2,512]{3,1,2,0:T(8,128)(2,1)} %rev.3), kind=kLoop, calls=%fused_computation.6 | loop fusion | flops 2097152 | bytes 8388608 | tf_op jit(solution)/shard_map/concatenate | solution.py:99
  149.1 11.2 %reshape.83 = bf16[8,8,32,2,8,64]{5,4,2,3,1,0:T(8,128)(2,1)} reshape(bf16[64,32,2,512]{3,1,2,0:T(8,128)(2,1)} %pad_maximum_fusion) | data formatting | bytes 8388608 | tf_op jit(solution)/shard_map/reshape | solution.py:101
  160.3 6.4 %gather_fusion.2 = bf16[4,8,32,2,8,64]{5,4,2,3,1,0:T(8,128)(2,1)} fusion(bf16[8,8,32,2,8,64]{5,4,2,3,1,0:T(8,128)(2,1)} %reshape.83, s32[1024]{0:T(1024)S(1)} %pad_clamp_fusion), kind=kCustom, calls=%fused_computation.1.clone | custom fusion | bytes 4194320 | tf_op jit(solution)/shard_map/jit(_take)/gather | solution.py:108
  166.7 6.4 %gather_fusion.1 = bf16[4,8,32,2,8,64]{5,4,2,3,1,0:T(8,128)(2,1)} fusion(bf16[8,8,32,2,8,64]{5,4,2,3,1,0:T(8,128)(2,1)} %reshape.83, s32[1024]{0:T(1024)S(1)} %pad_clamp_fusion.1), kind=kCustom, calls=%fused_computation.clone | custom fusion | bytes 4194320 | tf_op jit(solution)/shard_map/jit(_take)/gather | solution.py:108
  173.1 6.2 %broadcast_select_fusion = (bf16[4,8,32,2,8,64]{5,4,2,3,1,0:T(8,128)(2,1)S(1)}, bf16[4,8,32,2,8,64]{5,4,2,3,1,0:T(8,128)(2,1)}) fusion(bf16[4,8,32,2,8,64]{5,4,2,3,1,0:T(8,128)(2,1)} %gather_fusion.2, pred[4]{0:T(512)(128)(4,1)S(1)} %get-tuple-element.17, bf16[4,8,32,2,8,64]{5,4,2,3,1,0:T(8,128)(2,1)} %gather_fusion.1, pred[4]{0:T(512)(128)(4,1)S(1)} %get-tuple-element.6), kind=kLoop, calls=%fused_computation.11 | loop fusion | flops 2097152 | bytes 8388616 | tf_op jit(solution)/shard_map/jit(_take)/select_n | solution.py:108
  179.3 6.8 %copy.101 = bf16[4,8,32,2,8,64]{5,1,0,4,2,3:T(8,128)(2,1)} copy(bf16[4,8,32,2,8,64]{5,4,2,3,1,0:T(8,128)(2,1)S(1)} %get-tuple-element.25) | data formatting | bytes 4194304 | tf_op jit(solution)/shard_map/jit(_take)/select_n | solution.py:108
  186.1 3.0 %fusion.54 = (f32[32,8,8]{2,1,0:T(8,128)S(1)}, f32[32,8,8,32]{3,2,1,0:T(8,128)S(1)}) fusion(bf16[32,32,2,8,64]{4,0,3,1,2:T(8,128)(2,1)} %bitcast.125, bf16[8,32,8,64]{3,2,1,0:T(8,128)(2,1)S(1)} %reshape_squeeze.7), kind=kOutput, calls=%fused_computation.88 | convolution fusion | flops 8585247 | bytes 2629632 | tf_op jit(solution)/shard_map/sub | solution.py:26
  189.1 2.3 %fusion.29 = bf16[8,32,8,64]{3,0,2,1:T(8,128)(2,1)S(1)} fusion(bf16[32,32,2,8,64]{4,0,3,1,2:T(8,128)(2,1)} %bitcast.126, f32[32,8,8,32]{3,2,1,0:T(8,128)S(1)} %get-tuple-element.20, f32[32,8,8]{2,1,0:T(8,128)S(1)} %get-tuple-element.19), kind=kOutput, calls=%fused_computation.50 | convolution fusion | flops 8650752 | bytes 2629632 | tf_op jit(solution)/shard_map/lhqk,klhd->qlhd/dot_general | solution.py:120
  191.4 0.1 copy.73
  191.5 0.3 reshape.87
  191.8 9.2 %copy.102 = bf16[4,8,32,2,8,64]{5,1,0,4,2,3:T(8,128)(2,1)} copy(bf16[4,8,32,2,8,64]{5,4,2,3,1,0:T(8,128)(2,1)} %get-tuple-element.26) | data formatting | bytes 4194304 | tf_op jit(solution)/shard_map/jit(_take)/select_n | solution.py:108
  201.0 3.9 %fusion.55 = (f32[32,8,8]{2,1,0:T(8,128)S(1)}, f32[32,8,8,32]{3,2,1,0:T(8,128)}) fusion(bf16[32,32,2,8,64]{4,0,3,1,2:T(8,128)(2,1)} %bitcast.127, bf16[8,32,8,64]{3,2,1,0:T(8,128)(2,1)S(1)} %reshape_squeeze.6), kind=kOutput, calls=%fused_computation.89 | convolution fusion | flops 8585247 | bytes 2629632 | tf_op jit(solution)/shard_map/sub | solution.py:26
  204.9 2.7 %fusion.30 = bf16[8,32,8,64]{3,0,2,1:T(8,128)(2,1)S(1)} fusion(bf16[32,32,2,8,64]{4,0,3,1,2:T(8,128)(2,1)} %bitcast.128, f32[32,8,8,32]{3,2,1,0:T(8,128)} %get-tuple-element.22, f32[32,8,8]{2,1,0:T(8,128)S(1)} %get-tuple-element.21), kind=kOutput, calls=%fused_computation.51 | convolution fusion | flops 8650752 | bytes 3416064 | tf_op jit(solution)/shard_map/lhqk,klhd->qlhd/dot_general | solution.py:120
  207.6 0.9 copy.70
  208.5 2.2 %reshape.85 = bf16[8,32,512]{2,1,0:T(8,128)(2,1)} reshape(bf16[8,32,8,64]{3,2,1,0:T(8,128)(2,1)} %copy.70) | data formatting | bytes 524288 | tf_op jit(solution)/shard_map/reshape | solution.py:123
  210.7 1.7 fusion.33
  212.4 1.7 fusion.14
  (18 shorter events, 0.1 us)
Async XLA Ops:
  10.1 2.3 %copy-start.5 = (bf16[16,32,1024]{2,1,0:T(8,128)(2,1)S(1)}, bf16[16,32,1024]{2,1,0:T(8,128)(2,1)}, u32[]{:S(2)}) copy-start(bf16[16,32,1024]{2,1,0:T(8,128)(2,1)} %param.8) | copy-start | bytes 3145732
  10.1 2.3 %copy-start.7 = (f32[1024]{0:T(1024)S(1)}, f32[1024]{0:T(1024)}, u32[]{:S(2)}) copy-start(f32[1024]{0:T(1024)} %param.9) | copy-start | bytes 12292
  52.8 39.6 %all-to-all-start.1 = ((bf16[64,32,128]{2,1,0:T(8,128)(2,1)}), bf16[64,32,128]{2,1,0:T(8,128)(2,1)S(1)}, u32[]{:S(2)}, u32[]{:S(2)}) async-start(bf16[64,32,128]{2,1,0:T(8,128)(2,1)} %bitcast.9), calls=%async_computation.1 | async-start | bytes 1048576 | tf_op jit(solution)/shard_map/all_to_all | solution.py:76
  60.7 5.0 %copy-start.3 = (bf16[16,32,3,512]{3,1,2,0:T(8,128)(2,1)}, bf16[16,32,3,512]{3,1,2,0:T(8,128)(2,1)S(1)}, u32[]{:S(2)}) copy-start(bf16[16,32,3,512]{3,1,2,0:T(8,128)(2,1)S(1)} %fusion.18) | copy-start | bytes 4718596
  60.8 65.8 %collective-permute-start.2 = (bf16[16,32,2,512]{3,1,2,0:T(8,128)(2,1)S(1)}, bf16[16,32,2,512]{3,1,2,0:T(8,128)(2,1)}, u32[]{:S(2)}, u32[]{:S(2)}) collective-permute-start(bf16[16,32,2,512]{3,1,2,0:T(8,128)(2,1)S(1)} %slice.70), channel_id=1, source_target_pairs={{0,8},{8,0},{16,24},{24,16},{1,9},{9,1},{17,25},{25,17},{2,10},{10... | collective-permute-start | bytes 3145736 | tf_op jit(solution)/shard_map/ppermute | solution.py:21
  62.3 58.7 %collective-permute-start = (bf16[16,32,2,512]{3,1,2,0:T(8,128)(2,1)S(1)}, bf16[16,32,2,512]{3,1,2,0:T(8,128)(2,1)}, u32[]{:S(2)}, u32[]{:S(2)}) collective-permute-start(bf16[16,32,2,512]{3,1,2,0:T(8,128)(2,1)S(1)} %slice.70), channel_id=1, source_target_pairs={{0,4},{1,5},{2,6},{3,7},{4,0},{5,1},{6,2},{7,3},{8,12},{9,13},{10,... | collective-permute-start | bytes 3145736 | tf_op jit(solution)/shard_map/ppermute | solution.py:15
  97.5 3.3 %copy-start.4 = (bf16[8,256,2,64]{3,2,1,0:T(2,128)(2,1)S(1)}, bf16[8,256,2,64]{3,2,1,0:T(2,128)(2,1)}, u32[]{:S(2)}) copy-start(bf16[8,256,2,64]{3,2,1,0:T(2,128)(2,1)} %reshape.77) | copy-start | bytes 1572868
  102.4 27.5 %all-to-all-start.3 = ((bf16[8,256,128]{2,0,1:T(8,128)(2,1)}), bf16[8,256,128]{2,0,1:T(8,128)(2,1)S(1)}, u32[]{:S(2)}, u32[]{:S(2)}) async-start(bf16[8,256,128]{2,0,1:T(8,128)(2,1)} %copy.62), calls=%async_computation.3 | async-start | bytes 1048576 | tf_op jit(solution)/shard_map/all_to_all | solution.py:81
  121.0 9.8 %collective-permute-start.1 = (bf16[16,32,2,512]{3,1,2,0:T(8,128)(2,1)}, bf16[16,32,2,512]{3,1,2,0:T(8,128)(2,1)}, u32[]{:S(2)}, u32[]{:S(2)}) collective-permute-start(bf16[16,32,2,512]{3,1,2,0:T(8,128)(2,1)} %collective-permute-done), channel_id=1, source_target_pairs={{0,8},{8,0},{16,24},{24,16},{1,9},{9,1},{17,25},{25,17},{2,10},{10... | collective-permute-start | bytes 3145736 | tf_op jit(solution)/shard_map/ppermute | solution.py:21
  125.9 0.7 copy-start.6
  125.9 0.7 copy-start.8
  141.9 3.3 %copy-start = (bf16[32,32,2,512]{3,1,2,0:T(8,128)(2,1)S(1)}, bf16[32,32,2,512]{3,1,2,0:T(8,128)(2,1)}, u32[]{:S(2)}) copy-start(bf16[32,32,2,512]{3,1,2,0:T(8,128)(2,1)} %maximum_select_fusion.1) | copy-start | bytes 6291460
  204.9 5.8 %copy-start.1 = (bf16[1024,1024]{1,0:T(8,128)(2,1)S(1)}, bf16[1024,1024]{1,0:T(8,128)(2,1)}, u32[]{:S(2)}) copy-start(bf16[1024,1024]{1,0:T(8,128)(2,1)} %param.11) | copy-start | bytes 6291460
  208.5 3.9 %slice-start = ((bf16[1024,1024]{1,0:T(8,128)(2,1)}), bf16[512,1024]{1,0:T(8,128)(2,1)S(1)}, s32[]{:S(2)}) async-start(bf16[1024,1024]{1,0:T(8,128)(2,1)} %param.11), calls=%async_computation.4 | async-start | bytes 2097152 | tf_op jit(solution)/shard_map/slice | solution.py:125
  210.7 1.7 copy-start.2
where the time goes:
time: 215 us; the launch traced here: 214 us
  local copies, waits for them, and re-layouts  72.5 us (34%)
  waiting for transfers between devices  40.3 us (19%)
  blocking collectives  37.3 us (17%)
  other arithmetic  24.5 us (11%)
  matrix products  22.2 us (10%)
  starting transfers between devices  16.9 us (8%)
    all_to_all x1, waiting for transfers between devices, on_device(): lax.all_to_all(zonal_part[0], 'lon', split_axis=0, concat_axis=1, tiled=T...  26.7 us
    all_to_all x1, blocking collectives, on_device(): lax.all_to_all(zonal_part[1], 'lon', split_axis=0, concat_axis=1, tiled=T...  19.8 us
    all_to_all x1, blocking collectives, on_device(): lax.all_to_all(zonal_part[2], 'lon', split_axis=0, concat_axis=1, tiled=T...  17.5 us
    select_n x2, local copies, waits for them, and re-layouts, on_device(): jnp.take(column, picked, axis=0)  16 us
    ppermute x1, waiting for transfers between devices, shifted(): lax.ppermute(shard, axis, [(i, (i + by) % devices) for i in range(devices)])  13.7 us
    gather x2, local copies, waits for them, and re-layouts, on_device(): jnp.take(column, picked, axis=0)  12.8 us
    reshape x1, local copies, waits for them, and re-layouts, on_device(): column = column.reshape(block_total, BM, lon_count, 2, column_heads, HD)  11.2 us
    unnamed x19, local copies, waits for them, and re-layouts  8.72 us
  transfers between devices with their start and end apart: 5, of which 2 were waited for; matrix products, arithmetic and copies ran while one was open for 10% of the time, Pallas kernels for 0%

commit v1 on v0

--- a/solution.py
+++ b/solution.py
@@ -74,7 +74,12 @@
     ).astype(jnp.bfloat16)
     query_all, key_all, value_all = (
         lax.all_to_all(zonal_part[0], "lon", split_axis=0, concat_axis=1, tiled=True),
-        lax.all_to_all(zonal_part[1], "lon", split_axis=0, concat_axis=1, tiled=True),
+        jnp.concatenate(
+            lax.all_to_all(
+                jnp.stack(jnp.split(zonal_part[1], lax.axis_size("lon"), 0)), "lon", 0, 0
+            ),
+            1,
+        ),
         lax.all_to_all(zonal_part[2], "lon", split_axis=0, concat_axis=1, tiled=True),
     )
     zonal_items = zonal_attend(query_all, key_all, value_all)

time: 215 us -> 224 us (1.042)
  blocking collectives: 37.3 us -> 18.3 us
  waiting for transfers between devices: 40.3 us -> 57.7 us
  local copies, waits for them, and re-layouts: 72.5 us -> 80 us
  starting transfers between devices: 16.9 us -> 20.8 us
    all_to_all x2 -> x1, blocking collectives: 37.3 us -> 18.3 us  [on_device(): lax.all_to_all(zonal_part[0], 'lon', split_axis=0, concat_axis=1, tiled=T...]
    all_to_all x1, waiting for transfers between devices: 0.01 us -> 9.05 us  [on_device(): lax.all_to_all(zonal_items, 'lon', split_axis=1, concat_axis=0, tiled=True)]
    all_to_all x1 -> x2, waiting for transfers between devices: 26.7 us -> 34.9 us  [the longest x1 22.3 us: on_device(): lax.all_to_all(zonal_part[2], 'lon', split_axis=0, concat_axis=1, tiled=T...]
    all_to_all x1 -> x2, starting transfers between devices: 4.07 us -> 10.5 us  [the longest x1 6.37 us: on_device(): lax.all_to_all(jnp.stack(jnp.split(zonal_part[1], lax.axis_size('lon'), 0...]
    unnamed x19 -> x28, local copies, waits for them, and re-layouts: 8.72 us -> 14.2 us
    reshape x1, local copies, waits for them, and re-layouts: 2.44 us -> 0.04 us  [on_device(): jnp.concatenate(lax.all_to_all(jnp.stack(jnp.split(zonal_part[1], lax.axi...]
    select_n x1 -> x2, other arithmetic: 6.22 us -> 5.31 us  [on_device(): jnp.take(column, picked, axis=0)]
  transfers between devices with their start and end apart: 5 -> 6, of which waited for: 2 -> 4; matrix products, arithmetic and copies ran while one was open for 10% -> 11% of each run, Pallas kernels for 0% -> 0%
where the time goes in v1:
time: 224 us; the launch traced here: 222 us
  local copies, waits for them, and re-layouts  80 us (36%)
  waiting for transfers between devices  57.7 us (26%)
  other arithmetic  22.3 us (10%)
  matrix products  22.2 us (10%)
  starting transfers between devices  20.8 us (9%)
  blocking collectives  18.3 us (8%)
    all_to_all x1, waiting for transfers between devices, on_device(): lax.all_to_all(zonal_part[2], 'lon', split_axis=0, concat_axis=1, tiled=T...  22.3 us
    all_to_all x1, blocking collectives, on_device(): lax.all_to_all(zonal_part[0], 'lon', split_axis=0, concat_axis=1, tiled=T...  18.3 us
    unnamed x28, local copies, waits for them, and re-layouts  14.2 us
    select_n x2, local copies, waits for them, and re-layouts, on_device(): jnp.take(column, picked, axis=0)  13.9 us
    ppermute x1, waiting for transfers between devices, shifted(): lax.ppermute(shard, axis, [(i, (i + by) % devices) for i in range(devices)])  13.7 us
    gather x2, local copies, waits for them, and re-layouts, on_device(): jnp.take(column, picked, axis=0)  12.9 us
    all_to_all x1, waiting for transfers between devices, on_device(): lax.all_to_all(jnp.stack(jnp.split(zonal_part[1], lax.axis_size('lon'), 0...  12.5 us
    reshape x1, local copies, waits for them, and re-layouts, on_device(): column = column.reshape(block_total, BM, lon_count, 2, column_heads, HD)  11.2 us
  transfers between devices with their start and end apart: 6, of which 4 were waited for; matrix products, arithmetic and copies ran while one was open for 11% of the time, Pallas kernels for 0%

profile of v1, /device:TPU:1, one launch (start us, length us, event | category | flops | bytes accessed | tf_op | source)
XLA Modules:
  0.0 221.7 jit_solution(15346100354830885021)
XLA Ops:
  0.0 8.6 %copy.68 = bf16[1024,3072]{0,1:T(8,128)(2,1)} copy(bf16[1024,3072]{1,0:T(8,128)(2,1)} %param.10) | data formatting | bytes 12582912 | tf_op args[2]
  8.6 2.3 %slice.78 = bf16[1024,3,512]{0,2,1:T(8,128)(2,1)S(1)} slice(bf16[1024,3,1024]{0,2,1:T(8,128)(2,1)} %bitcast.128), slice={[0:1024], [0:3], [0:512]} | slice | bytes 6291456 | tf_op jit(solution)/shard_map/slice | solution.py:64
  10.9 0.3 fusion.7
  11.2 1.9 fusion.19
  13.2 0.6 constant_dynamic-update-slice_fusion.7
  13.8 0.6 constant_dynamic-update-slice_fusion.6
  14.5 0.6 constant_dynamic-update-slice_fusion.5
  15.1 0.6 constant_dynamic-update-slice_fusion.4
  15.7 0.6 constant_dynamic-update-slice_fusion.3
  16.4 0.6 constant_dynamic-update-slice_fusion.2
  17.0 0.6 constant_dynamic-update-slice_fusion.1
  17.6 0.6 constant_dynamic-update-slice_fusion
  18.3 6.4 %all-to-all-start.2 = ((bf16[8,8,32,128]{3,2,1,0:T(8,128)(2,1)}), bf16[8,8,32,128]{3,2,1,0:T(8,128)(2,1)S(1)}, u32[]{:S(2)}, u32[]{:S(2)}) async-start(bf16[8,8,32,128]{3,2,1,0:T(8,128)(2,1)} %constant_dynamic-update-slice_fusion), calls=%async_computation.2 | async-start | bytes 1048576 | tf_op jit(solution)/shard_map/all_to_all | solution.py:78
  24.6 0.9 fusion.52
  25.5 12.5 %all-to-all-done.2 = bf16[8,8,32,128]{3,2,1,0:T(8,128)(2,1)S(1)} async-done(((bf16[8,8,32,128]{3,2,1,0:T(8,128)(2,1)}), bf16[8,8,32,128]{3,2,1,0:T(8,128)(2,1)S(1)}, u32[]{:S(2)}, u32[]{:S(2)}) %all-to-all-start.2) | async-done | bytes 524320 | tf_op jit(solution)/shard_map/all_to_all | solution.py:78
  38.1 18.3 %all_to_all.50 = bf16[64,32,128]{2,1,0:T(8,128)(2,1)S(1)} all-to-all(bf16[64,32,128]{2,1,0:T(8,128)(2,1)S(1)} %bitcast.140), channel_id=1, replica_groups=mesh['lat'=4,'lon'=8] {'lon'}, dimensions={0} | all-to-all | bytes 1048576 | tf_op jit(solution)/shard_map/all_to_all | solution.py:76
  56.4 4.1 %all-to-all-start = ((bf16[64,32,128]{2,1,0:T(8,128)(2,1)}), bf16[64,32,128]{2,1,0:T(8,128)(2,1)}, u32[]{:S(2)}, u32[]{:S(2)}) async-start(bf16[64,32,128]{2,1,0:T(8,128)(2,1)} %bitcast.6), calls=%async_computation | async-start | bytes 1048576 | tf_op jit(solution)/shard_map/all_to_all | solution.py:83
  60.6 3.8 %fusion.18 = bf16[16,32,3,512]{3,1,2,0:T(8,128)(2,1)S(1)} fusion(bf16[1024,3,1024]{0,2,1:T(8,128)(2,1)} %bitcast.129, bf16[16,32,1024]{2,1,0:T(8,128)(2,1)S(1)} %copy-done.6, f32[1024]{0:T(1024)S(1)} %copy-done.8, f32[16,32]{1,0:T(8,128)S(1)} %add_rsqrt_fusion), kind=kOutput, calls=%fused_computation.38 | convolution fusion | flops 1613496320 | bytes 5773312 | tf_op jit(solution)/shard_map/rld,dtc->rltc/dot_general | solution.py:72
  64.4 0.1 slice.82
  64.5 1.0 copy-done.3
  65.5 2.3 %collective-permute-start = (bf16[16,32,2,512]{3,1,2,0:T(8,128)(2,1)S(1)}, bf16[16,32,2,512]{3,1,2,0:T(8,128)(2,1)}, u32[]{:S(2)}, u32[]{:S(2)}) collective-permute-start(bf16[16,32,2,512]{3,1,2,0:T(8,128)(2,1)S(1)} %slice.82), channel_id=1, source_target_pairs={{0,4},{1,5},{2,6},{3,7},{4,0},{5,1},{6,2},{7,3},{8,12},{9,13},{10,... | collective-permute-start | bytes 3145736 | tf_op jit(solution)/shard_map/ppermute | solution.py:15
  67.8 2.3 %collective-permute-start.2 = (bf16[16,32,2,512]{3,1,2,0:T(8,128)(2,1)S(1)}, bf16[16,32,2,512]{3,1,2,0:T(8,128)(2,1)}, u32[]{:S(2)}, u32[]{:S(2)}) collective-permute-start(bf16[16,32,2,512]{3,1,2,0:T(8,128)(2,1)S(1)} %slice.82), channel_id=1, source_target_pairs={{0,8},{8,0},{16,24},{24,16},{1,9},{9,1},{17,25},{25,17},{2,10},{10... | collective-permute-start | bytes 3145736 | tf_op jit(solution)/shard_map/ppermute | solution.py:21
  70.1 0.4 reshape_reshape.3
  70.5 0.8 copy.71
  71.4 2.4 %reshape.93 = bf16[8,256,2,64]{3,2,1,0:T(2,128)(2,1)S(1)} reshape(bf16[8,8,32,128]{3,2,1,0:T(8,128)(2,1)} %copy.71) | data formatting | bytes 1048576 | tf_op jit(solution)/shard_map/reshape | solution.py:33
  73.8 22.3 %all-to-all-done = bf16[64,32,128]{2,1,0:T(8,128)(2,1)} async-done(((bf16[64,32,128]{2,1,0:T(8,128)(2,1)}), bf16[64,32,128]{2,1,0:T(8,128)(2,1)}, u32[]{:S(2)}, u32[]{:S(2)}) %all-to-all-start) | async-done | bytes 524320 | tf_op jit(solution)/shard_map/all_to_all | solution.py:83
  96.2 1.9 copy.70
  98.0 3.2 %reshape.92 = bf16[8,256,2,64]{3,2,1,0:T(2,128)(2,1)} reshape(bf16[8,8,32,128]{3,2,1,0:T(8,128)(2,1)} %copy.70) | data formatting | bytes 1048576 | tf_op jit(solution)/shard_map/reshape | solution.py:35
  101.2 0.7 fusion.36
  101.9 3.2 %fusion.57 = (f32[8,2,256]{2,1,0:T(2,128)S(1)}, f32[8,2,256,256]{2,3,1,0:T(8,128)S(1)}) fusion(f32[8,2,256,256]{2,3,1,0:T(8,128)S(1)} %fusion.36), kind=kOutput, calls=%fused_computation.99 | output fusion | flops 4194559 | bytes 8404992 | tf_op jit(solution)/shard_map/sub | solution.py:26
  105.2 13.7 %collective-permute-done = bf16[16,32,2,512]{3,1,2,0:T(8,128)(2,1)} collective-permute-done((bf16[16,32,2,512]{3,1,2,0:T(8,128)(2,1)S(1)}, bf16[16,32,2,512]{3,1,2,0:T(8,128)(2,1)}, u32[]{:S(2)}, u32[]{:S(2)}) %collective-permute-start) | collective-permute-done | bytes 1048608 | tf_op jit(solution)/shard_map/ppermute | solution.py:15
  118.9 2.1 collective-permute-start.1
  121.0 0.5 fusion.28
  121.6 1.1 copy.77
  122.6 3.7 %all-to-all-start.3 = ((bf16[8,256,128]{2,0,1:T(8,128)(2,1)}), bf16[8,256,128]{2,0,1:T(8,128)(2,1)S(1)}, u32[]{:S(2)}, u32[]{:S(2)}) async-start(bf16[8,256,128]{2,0,1:T(8,128)(2,1)} %copy.77), calls=%async_computation.3 | async-start | bytes 1048576 | tf_op jit(solution)/shard_map/all_to_all | solution.py:86
  126.3 1.1 fusion.54
  127.4 0.3 reshape_squeeze.6
  127.7 0.3 reshape_squeeze.7
  128.0 0.1 copy-done.7
  128.2 3.2 %maximum_select_fusion.1 = bf16[32,32,2,512]{3,1,2,0:T(8,128)(2,1)} fusion(bf16[16,32,2,512]{3,1,2,0:T(8,128)(2,1)} %collective-permute-done.2, bf16[16,32,2,512]{3,1,2,0:T(8,128)(2,1)S(1)} %slice.82, pred[]{:T(512)S(6)} %eq.8), kind=kLoop, calls=%fused_computation.31 | loop fusion | flops 3145728 | bytes 4194305 | tf_op jit(solution)/shard_map/jit(_where)/select_n | solution.py:93
  131.4 9.0 %all-to-all-done.3 = bf16[8,256,128]{2,0,1:T(8,128)(2,1)S(1)} async-done(((bf16[8,256,128]{2,0,1:T(8,128)(2,1)}), bf16[8,256,128]{2,0,1:T(8,128)(2,1)S(1)}, u32[]{:S(2)}, u32[]{:S(2)}) %all-to-all-start.3) | async-done | bytes 524320 | tf_op jit(solution)/shard_map/all_to_all | solution.py:86
  140.4 0.9 copy.79
  141.4 2.6 %maximum_select_fusion = bf16[32,32,2,512]{3,1,2,0:T(8,128)(2,1)S(1)} fusion(bf16[16,32,2,512]{3,1,2,0:T(8,128)(2,1)} %collective-permute-done.1, bf16[16,32,2,512]{3,1,2,0:T(8,128)(2,1)} %collective-permute-done, pred[]{:T(512)S(6)} %eq.8), kind=kLoop, calls=%fused_computation.30 | loop fusion | flops 3145728 | bytes 4194305 | tf_op jit(solution)/shard_map/jit(_where)/select_n | solution.py:93
  143.9 2.5 %copy.81 = bf16[32,32,2,512]{3,0,2,1:T(8,128)(2,1)} copy(bf16[32,32,2,512]{3,1,2,0:T(8,128)(2,1)S(1)} %maximum_select_fusion) | data formatting | bytes 4194304 | tf_op jit(solution)/shard_map/jit(_where)/select_n | solution.py:93
  146.4 2.3 %gather_fusion = bf16[32,32,2,512]{3,1,2,0:T(8,128)(2,1)S(1)} fusion(bf16[32,32,2,512]{3,0,2,1:T(8,128)(2,1)} %copy.81, s32[1024]{0:T(1024)S(1)} %pad_clamp_fusion.2), kind=kCustom, calls=%fused_computation.2 | custom fusion | bytes 4194432 | tf_op jit(solution)/shard_map/jit(_take)/gather | solution.py:103
  148.7 3.7 %fusion.15 = bf16[32,32,2,512]{3,1,2,0:T(8,128)(2,1)} fusion(bf16[32,32,2,512]{3,1,2,0:T(8,128)(2,1)S(1)} %gather_fusion, pred[32]{0:T(512)(128)(4,1)S(1)} %get-tuple-element.10), kind=kLoop, calls=%fused_computation.35 | loop fusion | flops 1048576 | bytes 4194336 | tf_op jit(solution)/shard_map/jit(_take)/select_n | solution.py:103
  152.4 3.3 %rev.3 = bf16[32,32,2,512]{3,1,2,0:T(8,128)(2,1)} reverse(bf16[32,32,2,512]{3,1,2,0:T(8,128)(2,1)} %fusion.15), dimensions={0} | reverse | bytes 4194304 | tf_op jit(solution)/shard_map/rev | solution.py:103
  155.8 3.9 %pad_maximum_fusion = bf16[64,32,2,512]{3,1,2,0:T(8,128)(2,1)} fusion(bf16[32,32,2,512]{3,1,2,0:T(8,128)(2,1)S(1)} %copy-done, bf16[32,32,2,512]{3,1,2,0:T(8,128)(2,1)} %rev.3), kind=kLoop, calls=%fused_computation.6 | loop fusion | flops 2097152 | bytes 8388608 | tf_op jit(solution)/shard_map/concatenate | solution.py:104
  159.7 11.2 %reshape.98 = bf16[8,8,32,2,8,64]{5,4,2,3,1,0:T(8,128)(2,1)} reshape(bf16[64,32,2,512]{3,1,2,0:T(8,128)(2,1)} %pad_maximum_fusion) | data formatting | bytes 8388608 | tf_op jit(solution)/shard_map/reshape | solution.py:106
  170.9 6.4 %gather_fusion.1 = bf16[4,8,32,2,8,64]{5,4,2,3,1,0:T(8,128)(2,1)} fusion(bf16[8,8,32,2,8,64]{5,4,2,3,1,0:T(8,128)(2,1)} %reshape.98, s32[1024]{0:T(1024)S(1)} %get-tuple-element.33), kind=kCustom, calls=%fused_computation.clone | custom fusion | bytes 4194320 | tf_op jit(solution)/shard_map/jit(_take)/gather | solution.py:113
  177.3 2.7 %broadcast_select_fusion.1 = bf16[4,8,32,2,8,64]{5,4,2,3,1,0:T(8,128)(2,1)S(1)} fusion(bf16[4,8,32,2,8,64]{5,4,2,3,1,0:T(8,128)(2,1)} %gather_fusion.1, pred[4]{0:T(512)(128)(4,1)S(1)} %get-tuple-element.6), kind=kLoop, calls=%fused_computation.12 | loop fusion | flops 1048576 | bytes 4194308 | tf_op jit(solution)/shard_map/jit(_take)/select_n | solution.py:113
  180.0 6.8 %copy.117 = bf16[4,8,32,2,8,64]{5,1,0,4,2,3:T(8,128)(2,1)} copy(bf16[4,8,32,2,8,64]{5,4,2,3,1,0:T(8,128)(2,1)S(1)} %broadcast_select_fusion.1) | data formatting | bytes 4194304 | tf_op jit(solution)/shard_map/jit(_take)/select_n | solution.py:113
  186.8 3.0 %fusion.56 = (f32[32,8,8]{2,1,0:T(8,128)S(1)}, f32[32,8,8,32]{3,2,1,0:T(8,128)S(1)}) fusion(bf16[32,32,2,8,64]{4,0,3,1,2:T(8,128)(2,1)} %bitcast.130, bf16[8,32,8,64]{3,2,1,0:T(8,128)(2,1)S(1)} %reshape_squeeze.6), kind=kOutput, calls=%fused_computation.98 | convolution fusion | flops 8585247 | bytes 2629632 | tf_op jit(solution)/shard_map/sub | solution.py:26
  189.8 2.3 %fusion.30 = bf16[8,32,8,64]{3,0,2,1:T(8,128)(2,1)S(1)} fusion(bf16[32,32,2,8,64]{4,0,3,1,2:T(8,128)(2,1)} %bitcast.131, f32[32,8,8,32]{3,2,1,0:T(8,128)S(1)} %get-tuple-element.29, f32[32,8,8]{2,1,0:T(8,128)S(1)} %get-tuple-element.28), kind=kOutput, calls=%fused_computation.51 | convolution fusion | flops 8650752 | bytes 2629632 | tf_op jit(solution)/shard_map/lhqk,klhd->qlhd/dot_general | solution.py:125
  192.2 0.3 reshape.100
  192.5 6.4 %gather_fusion.2 = bf16[4,8,32,2,8,64]{5,4,2,3,1,0:T(8,128)(2,1)} fusion(bf16[8,8,32,2,8,64]{5,4,2,3,1,0:T(8,128)(2,1)} %reshape.98, s32[1024]{0:T(1024)S(1)} %get-tuple-element.32), kind=kCustom, calls=%fused_computation.1.clone | custom fusion | bytes 4194320 | tf_op jit(solution)/shard_map/jit(_take)/gather | solution.py:113
  198.9 2.7 %broadcast_select_fusion = bf16[4,8,32,2,8,64]{5,4,2,3,1,0:T(8,128)(2,1)S(1)} fusion(bf16[4,8,32,2,8,64]{5,4,2,3,1,0:T(8,128)(2,1)} %gather_fusion.2, pred[4]{0:T(512)(128)(4,1)S(1)} %get-tuple-element.24), kind=kLoop, calls=%fused_computation.11 | loop fusion | flops 1048576 | bytes 4194308 | tf_op jit(solution)/shard_map/jit(_take)/select_n | solution.py:113
  201.6 7.1 %copy.116 = bf16[4,8,32,2,8,64]{5,1,0,4,2,3:T(8,128)(2,1)} copy(bf16[4,8,32,2,8,64]{5,4,2,3,1,0:T(8,128)(2,1)S(1)} %broadcast_select_fusion) | data formatting | bytes 4194304 | tf_op jit(solution)/shard_map/jit(_take)/select_n | solution.py:113
  208.6 3.9 %fusion.55 = (f32[32,8,8]{2,1,0:T(8,128)S(1)}, f32[32,8,8,32]{3,2,1,0:T(8,128)}) fusion(bf16[32,32,2,8,64]{4,0,3,1,2:T(8,128)(2,1)} %bitcast.132, bf16[8,32,8,64]{3,2,1,0:T(8,128)(2,1)S(1)} %reshape_squeeze.7), kind=kOutput, calls=%fused_computation.97 | convolution fusion | flops 8585247 | bytes 2629632 | tf_op jit(solution)/shard_map/sub | solution.py:26
  212.5 2.7 %fusion.29 = bf16[8,32,8,64]{3,0,2,1:T(8,128)(2,1)S(1)} fusion(bf16[32,32,2,8,64]{4,0,3,1,2:T(8,128)(2,1)} %bitcast.133, f32[32,8,8,32]{3,2,1,0:T(8,128)} %get-tuple-element.27, f32[32,8,8]{2,1,0:T(8,128)S(1)} %get-tuple-element.26), kind=kOutput, calls=%fused_computation.50 | convolution fusion | flops 8650752 | bytes 3416064 | tf_op jit(solution)/shard_map/lhqk,klhd->qlhd/dot_general | solution.py:125
  215.2 0.9 copy.88
  216.1 2.2 reshape.102
  218.3 1.7 fusion.33
  220.0 1.7 fusion.14
  (30 shorter events, 0.2 us)
Async XLA Ops:
  8.6 2.3 %copy-start.5 = (bf16[16,32,1024]{2,1,0:T(8,128)(2,1)S(1)}, bf16[16,32,1024]{2,1,0:T(8,128)(2,1)}, u32[]{:S(2)}) copy-start(bf16[16,32,1024]{2,1,0:T(8,128)(2,1)} %param.8) | copy-start | bytes 3145732
  8.6 2.6 %copy-start.8 = (f32[1024]{0:T(1024)S(1)}, f32[1024]{0:T(1024)}, u32[]{:S(2)}) copy-start(f32[1024]{0:T(1024)} %param.9) | copy-start | bytes 12292
  18.3 19.8 %all-to-all-start.2 = ((bf16[8,8,32,128]{3,2,1,0:T(8,128)(2,1)}), bf16[8,8,32,128]{3,2,1,0:T(8,128)(2,1)S(1)}, u32[]{:S(2)}, u32[]{:S(2)}) async-start(bf16[8,8,32,128]{3,2,1,0:T(8,128)(2,1)} %constant_dynamic-update-slice_fusion), calls=%async_computation.2 | async-start | bytes 1048576 | tf_op jit(solution)/shard_map/all_to_all | solution.py:78
  25.5 35.0 %copy-start.6 = (bf16[16,32,1024]{2,1,0:T(8,128)(2,1)S(1)}, bf16[16,32,1024]{2,1,0:T(8,128)(2,1)}, u32[]{:S(2)}) copy-start(bf16[16,32,1024]{2,1,0:T(8,128)(2,1)} %param.8) | copy-start | bytes 3145732
  56.4 39.8 %all-to-all-start = ((bf16[64,32,128]{2,1,0:T(8,128)(2,1)}), bf16[64,32,128]{2,1,0:T(8,128)(2,1)}, u32[]{:S(2)}, u32[]{:S(2)}) async-start(bf16[64,32,128]{2,1,0:T(8,128)(2,1)} %bitcast.6), calls=%async_computation | async-start | bytes 1048576 | tf_op jit(solution)/shard_map/all_to_all | solution.py:83
  64.4 1.1 copy-start.3
  65.5 53.4 %collective-permute-start = (bf16[16,32,2,512]{3,1,2,0:T(8,128)(2,1)S(1)}, bf16[16,32,2,512]{3,1,2,0:T(8,128)(2,1)}, u32[]{:S(2)}, u32[]{:S(2)}) collective-permute-start(bf16[16,32,2,512]{3,1,2,0:T(8,128)(2,1)S(1)} %slice.82), channel_id=1, source_target_pairs={{0,4},{1,5},{2,6},{3,7},{4,0},{5,1},{6,2},{7,3},{8,12},{9,13},{10,... | collective-permute-start | bytes 3145736 | tf_op jit(solution)/shard_map/ppermute | solution.py:15
  67.8 60.4 %collective-permute-start.2 = (bf16[16,32,2,512]{3,1,2,0:T(8,128)(2,1)S(1)}, bf16[16,32,2,512]{3,1,2,0:T(8,128)(2,1)}, u32[]{:S(2)}, u32[]{:S(2)}) collective-permute-start(bf16[16,32,2,512]{3,1,2,0:T(8,128)(2,1)S(1)} %slice.82), channel_id=1, source_target_pairs={{0,8},{8,0},{16,24},{24,16},{1,9},{9,1},{17,25},{25,17},{2,10},{10... | collective-permute-start | bytes 3145736 | tf_op jit(solution)/shard_map/ppermute | solution.py:21
  101.9 19.1 %copy-start.4 = (bf16[8,256,2,64]{3,2,1,0:T(2,128)(2,1)S(1)}, bf16[8,256,2,64]{3,2,1,0:T(2,128)(2,1)}, u32[]{:S(2)}) copy-start(bf16[8,256,2,64]{3,2,1,0:T(2,128)(2,1)} %reshape.92) | copy-start | bytes 1572868
  118.9 22.4 %collective-permute-start.1 = (bf16[16,32,2,512]{3,1,2,0:T(8,128)(2,1)}, bf16[16,32,2,512]{3,1,2,0:T(8,128)(2,1)}, u32[]{:S(2)}, u32[]{:S(2)}) collective-permute-start(bf16[16,32,2,512]{3,1,2,0:T(8,128)(2,1)} %collective-permute-done), channel_id=1, source_target_pairs={{0,8},{8,0},{16,24},{24,16},{1,9},{9,1},{17,25},{25,17},{2,10},{10... | collective-permute-start | bytes 3145736 | tf_op jit(solution)/shard_map/ppermute | solution.py:21
  122.6 17.8 %all-to-all-start.3 = ((bf16[8,256,128]{2,0,1:T(8,128)(2,1)}), bf16[8,256,128]{2,0,1:T(8,128)(2,1)S(1)}, u32[]{:S(2)}, u32[]{:S(2)}) async-start(bf16[8,256,128]{2,0,1:T(8,128)(2,1)} %copy.77), calls=%async_computation.3 | async-start | bytes 1048576 | tf_op jit(solution)/shard_map/all_to_all | solution.py:86
  127.4 0.7 copy-start.7
  127.4 0.7 copy-start.9
  152.4 3.3 %copy-start = (bf16[32,32,2,512]{3,1,2,0:T(8,128)(2,1)S(1)}, bf16[32,32,2,512]{3,1,2,0:T(8,128)(2,1)}, u32[]{:S(2)}) copy-start(bf16[32,32,2,512]{3,1,2,0:T(8,128)(2,1)} %maximum_select_fusion.1) | copy-start | bytes 6291460
  212.5 5.8 %copy-start.1 = (bf16[1024,1024]{1,0:T(8,128)(2,1)S(1)}, bf16[1024,1024]{1,0:T(8,128)(2,1)}, u32[]{:S(2)}) copy-start(bf16[1024,1024]{1,0:T(8,128)(2,1)} %param.11) | copy-start | bytes 6291460
  216.1 3.9 %slice-start = ((bf16[1024,1024]{1,0:T(8,128)(2,1)}), bf16[512,1024]{1,0:T(8,128)(2,1)S(1)}, s32[]{:S(2)}) async-start(bf16[1024,1024]{1,0:T(8,128)(2,1)} %param.11), calls=%async_computation.4 | async-start | bytes 2097152 | tf_op jit(solution)/shard_map/slice | solution.py:130
  218.3 1.7 copy-start.2
